TPU v7x, 32 devices: a whole 2x2x4 slice. The times are simulated.
32 devices in a mesh: groups: 2 (over x), shot: 16 (over z, y, core).
Axes of the slice: x: 2, y: 2, z: 4, core: 2. Of those that a mesh axis runs over, the one named last changes fastest.
Arguments:
- forward_state: float32 [32, 13, 16, 64, 128], P(('groups', 'shot')), parts along dimension 0, may hold values from -6 to 6
- adjoint_state: float32 [32, 13, 16, 64, 128], P(('groups', 'shot')), parts along dimension 0, may hold values from -6 to 6
- source_amp: float32 [32, 2], P(('groups', 'shot')), parts along dimension 0, may hold values from -12 to 12
- source_cell: int32 [32], P(('groups', 'shot')), parts along dimension 0, may hold values from 0 to 131071
- receiver_cells: int32 [32, 1024], P(('groups', 'shot')), parts along dimension 0, may hold values from 0 to 131071
- recorded: float32 [32, 1024], P(('groups', 'shot')), parts along dimension 0, may hold values from -6 to 6
- material: float32 [4, 32, 64, 128], P(None, 'groups', 'shot'), parts along dimension 1, may hold values from 0.3 to 2
- cell_class: int32 [32, 64, 128], P('groups'), parts along dimension 0, may hold values from 0 to 3
- class_factors: float32 [4, 4], replicated, may hold values from 0.5 to 2
Outputs:
- gradient: float32 [4, 32, 64, 128], P(None, 'groups', 'shot'), parts along dimension 1
There are 2 independent parts, one for each index of `groups`. A program takes and returns all parts, laid end to end along the dimension named above; an argument that names none is the same for every part. Nothing has to cross between parts.
All inputs are finite; a program needn't handle non-finite values.
Results may differ from a plain program's by a relative error of at most 0.00002.
Values sent between devices are 32-bit elements; how exact they have to be, the bound alone decides.
A program may use at most 128 MiB of HBM per device.

v0:
```python
import jax
import jax.numpy as jnp
from jax import lax
from jax.sharding import PartitionSpec as P

BIOT_COEFF = 0.8
RHO_BULK = 2.2
RHO_FLUID = 1.0
MASS_FLUID = 2.5
TIME_STEP = 0.25


def forward_diff(field, axis):
    count = field.shape[axis]
    ahead = jnp.concatenate(
        [
            lax.slice_in_dim(field, 1, count, axis=axis),
            jnp.zeros_like(lax.slice_in_dim(field, 0, 1, axis=axis)),
        ],
        axis=axis,
    )
    return ahead - field


def backward_diff(field, axis):
    count = field.shape[axis]
    behind = jnp.concatenate(
        [
            jnp.zeros_like(lax.slice_in_dim(field, 0, 1, axis=axis)),
            lax.slice_in_dim(field, 0, count - 1, axis=axis),
        ],
        axis=axis,
    )
    return field - behind


def advance(state, model, amplitude, source):
    vel_x, vel_z, vel_y, flux_x, flux_z, flux_y = (
        state[0],
        state[1],
        state[2],
        state[3],
        state[4],
        state[5],
    )
    sig_xx, sig_zz, sig_yy, sig_xz, sig_xy, sig_zy, pressure = (
        state[6],
        state[7],
        state[8],
        state[9],
        state[10],
        state[11],
        state[12],
    )
    lame_first, shear_mod, biot_mod, damping = (model[0], model[1], model[2], model[3])
    determinant = RHO_BULK * MASS_FLUID - RHO_FLUID * RHO_FLUID
    force_x = forward_diff(sig_xx, 0) + backward_diff(sig_xz, 1) + backward_diff(sig_xy, 2)
    force_z = backward_diff(sig_xz, 0) + forward_diff(sig_zz, 1) + backward_diff(sig_zy, 2)
    force_y = backward_diff(sig_xy, 0) + backward_diff(sig_zy, 1) + forward_diff(sig_yy, 2)
    drag_x = -forward_diff(pressure, 0) - damping * flux_x
    drag_z = -forward_diff(pressure, 1) - damping * flux_z
    drag_y = -forward_diff(pressure, 2) - damping * flux_y
    vel_x = vel_x + TIME_STEP * (MASS_FLUID * force_x - RHO_FLUID * drag_x) / determinant
    vel_z = vel_z + TIME_STEP * (MASS_FLUID * force_z - RHO_FLUID * drag_z) / determinant
    vel_y = vel_y + TIME_STEP * (MASS_FLUID * force_y - RHO_FLUID * drag_y) / determinant
    flux_x = flux_x + TIME_STEP * (RHO_BULK * drag_x - RHO_FLUID * force_x) / determinant
    flux_z = flux_z + TIME_STEP * (RHO_BULK * drag_z - RHO_FLUID * force_z) / determinant
    flux_y = flux_y + TIME_STEP * (RHO_BULK * drag_y - RHO_FLUID * force_y) / determinant
    strain_xx = backward_diff(vel_x, 0)
    strain_zz = backward_diff(vel_z, 1)
    strain_yy = backward_diff(vel_y, 2)
    div_solid = strain_xx + strain_zz + strain_yy
    div_flux = backward_diff(flux_x, 0) + backward_diff(flux_z, 1) + backward_diff(flux_y, 2)
    strain_xz = 0.5 * (forward_diff(vel_x, 1) + forward_diff(vel_z, 0))
    strain_xy = 0.5 * (forward_diff(vel_x, 2) + forward_diff(vel_y, 0))
    strain_zy = 0.5 * (forward_diff(vel_z, 2) + forward_diff(vel_y, 1))
    bulk_term = (
        lame_first + BIOT_COEFF * BIOT_COEFF * biot_mod
    ) * div_solid + BIOT_COEFF * biot_mod * div_flux
    sig_xx = sig_xx + TIME_STEP * (2.0 * shear_mod * strain_xx + bulk_term)
    sig_zz = sig_zz + TIME_STEP * (2.0 * shear_mod * strain_zz + bulk_term)
    sig_yy = sig_yy + TIME_STEP * (2.0 * shear_mod * strain_yy + bulk_term)
    sig_xz = sig_xz + TIME_STEP * 2.0 * shear_mod * strain_xz
    sig_xy = sig_xy + TIME_STEP * 2.0 * shear_mod * strain_xy
    sig_zy = sig_zy + TIME_STEP * 2.0 * shear_mod * strain_zy
    pressure = pressure - TIME_STEP * biot_mod * (BIOT_COEFF * div_solid + div_flux)
    pressure = pressure.reshape(-1).at[source].add(amplitude).reshape(pressure.shape)
    return jnp.stack(
        [
            vel_x,
            vel_z,
            vel_y,
            flux_x,
            flux_z,
            flux_y,
            sig_xx,
            sig_zz,
            sig_yy,
            sig_xz,
            sig_xy,
            sig_zy,
            pressure,
        ]
    )


def shot_gradient(model, start_state, adjoint, amplitudes, source, receivers, observed):

    def march(params):
        state = start_state
        for section in range(2):
            state = advance(state, params, amplitudes[section], source)
        return state

    final, pullback = jax.vjp(march, model)
    misfit = final[12].reshape(-1)[receivers] - observed
    pressure_cot = adjoint[12].reshape(-1).at[receivers].add(misfit).reshape(adjoint[12].shape)
    cotangent = adjoint.at[12].set(pressure_cot)
    return pullback(cotangent)[0]


def class_factor_map(cell_class, class_factors):
    classes = jnp.arange(class_factors.shape[1], dtype=jnp.int32)
    onehot = (cell_class[None] == classes[:, None, None, None]).astype(jnp.float32)
    return jnp.sum(class_factors[:, :, None, None, None] * onehot[None], axis=1)


def per_device(
    forward_state,
    adjoint_state,
    source_amp,
    source_cell,
    receiver_cells,
    recorded,
    material,
    cell_class,
    class_factors,
):
    whole_model = lax.all_gather(material, "shot", axis=2, tiled=True)
    factor = class_factor_map(cell_class, class_factors)
    model = whole_model * factor
    total = shot_gradient(
        model,
        forward_state[0],
        adjoint_state[0],
        source_amp[0],
        source_cell[0],
        receiver_cells[0],
        recorded[0],
    )
    piece = material.shape[2]
    offset = lax.axis_index("shot") * piece
    own_factor = lax.dynamic_slice_in_dim(factor, offset, piece, 2)
    summed = lax.psum_scatter(total, "shot", scatter_dimension=2, tiled=True)
    shot_count = forward_state.shape[0] * lax.axis_size("shot")
    return summed * own_factor / jnp.sqrt(jnp.float32(shot_count))


def solution(mesh):
    placed = (
        P(("groups", "shot"), None, None, None, None),
        P(("groups", "shot"), None, None, None, None),
        P(("groups", "shot"), None),
        P(("groups", "shot")),
        P(("groups", "shot"), None),
        P(("groups", "shot"), None),
        P(None, "groups", "shot", None),
        P("groups", None, None),
        P(),
    )
    return jax.shard_map(
        per_device,
        mesh=mesh,
        in_specs=placed,
        out_specs=P(None, "groups", "shot", None),
        check_vma=False,
    )
```

profile of v0, /device:TPU:0, one launch (start us, length us, event | category | flops | bytes accessed | tf_op | source)
XLA Modules:
  0.0 216.4 jit_solution(12800307589891833662)
XLA Ops:
  6.5 1.6 copy.50
  8.2 3.0 %slice_bitcast_fusion.10 = (f32[16,64,128]{2,1,0:T(8,128)S(1)}, f32[16,64,128]{2,1,0:T(8,128)S(1)}, f32[16,64,128]{2,1,0:T(8,128)S(1)}, f32[16,64,128]{2,1,0:T(8...) fusion(f32[1,13,16,64,128]{4,3,2,1,0:T(8,128)} %param.15), kind=kLoop, calls=%fused_computation.250 | loop fusion | bytes 6291456 | tf_op jit(solution)/shard_map/jvp()/squeeze | solution.py:49
  11.2 0.9 slice.388
  12.1 1.0 slice.392
  13.7 1.0 slice.391
  14.8 0.8 slice.386
  15.6 0.6 fusion.154
  16.2 1.3 fusion
  17.6 2.0 multiply_reduce_fusion
  19.6 2.9 %slice_bitcast_fusion.16 = (f32[15,64,128]{2,1,0:T(8,128)}, f32[15,64,128]{2,1,0:T(8,128)}, f32[15,64,128]{2,1,0:T(8,128)}, f32[15,64,128]{2,1,0:T(8,128)}) fusion(f32[1,13,16,64,128]{4,3,2,1,0:T(8,128)} %param.15), kind=kLoop, calls=%fused_computation.264 | loop fusion | bytes 3932160 | tf_op jit(solution)/shard_map/jvp()/slice | solution.py:30
  22.5 31.2 %all-gather.2.cloned.1.call-done = f32[4,16,64,128]{3,1,0,2:T(8,128)} async-done(((f32[4,16,4,128]{3,1,0,2:T(8,128)}), f32[4,16,64,128]{3,1,0,2:T(8,128)}) %all-gather.2.cloned.1.call-update) | async-done | bytes 2097168 | tf_op jit(solution)/shard_map/all_gather | solution.py:139
  53.7 3.6 %copy_multiply_fusion = f32[4,16,64,128]{3,2,1,0:T(8,128)S(1)} fusion(f32[4,16,64,128]{3,2,1,0:T(8,128)} %multiply_reduce_fusion, f32[4,16,64,128]{3,1,0,2:T(8,128)} %all-gather.2.cloned.1.call-done), kind=kLoop, calls=%fused_computation.4 | loop fusion | flops 524288 | bytes 6291456 | tf_op jit(solution)/shard_map/mul | solution.py:141
  57.4 3.1 %bitcast_add_fusion.12 = (f32[16,64,128]{2,1,0:T(8,128)S(1)}, f32[16,64,128]{2,1,0:T(8,128)S(1)}, f32[16,64,128]{2,1,0:T(8,128)S(1)}) fusion(f32[1,13,16,64,128]{4,3,2,1,0:T(8,128)} %param.15, f32[4,16,64,128]{3,2,1,0:T(8,128)S(1)} %copy_multiply_fusion, f32[16,64,127]{2,1,0:T(8,128)} %slice.392, f32[16,64,127]{2,1,0:T(8,128)} %slice.391, ...), kind=kLoop, calls=%fused_computation.187 | loop fusion | flops 1703936 | bytes 7290880 | tf_op jit(solution)/shard_map/jvp()/add | solution.py:65
  60.7 0.7 bitcast_add_fusion.16
  62.0 0.6 bitcast_add_fusion.14
  62.9 0.5 bitcast_add_fusion.11
  63.5 1.0 fusion.107
  64.5 0.5 fusion.110
  65.1 0.9 fusion.132
  66.3 2.2 %fusion.96 = (f32[16,64,128]{2,1,0:T(8,128)S(1)}, f32[16,64,128]{2,1,0:T(8,128)}, f32[16,64,128]{2,1,0:T(8,128)S(1)}, f32[16,64,128]{2,1,0:T(8,128)}, f32[16,64,...) fusion(f32[4,16,64,128]{3,2,1,0:T(8,128)S(1)} %copy_multiply_fusion, ...), kind=kLoop, calls=%fused_computation.148 | loop fusion | flops 3276800 | bytes 11964416 | tf_op jit(solution)/shard_map/jvp()/add | solution.py:83
  68.6 0.7 multiply_add_fusion.11
  69.4 1.0 slice.427
  70.4 1.0 slice.425
  71.6 0.9 multiply_add_fusion.10
  72.5 0.9 multiply_add_fusion.9
  73.4 0.9 slice.426
  74.3 0.9 slice.424
  75.2 0.9 slice.428
  76.1 1.1 slice.423
  77.5 1.9 fusion.126
  79.4 2.1 fusion.133
  81.5 12.6 %gather_fusion = f32[1024]{0:T(1024)S(1)} fusion(f32[131072]{0:T(1024)} %fusion.133, s32[1024]{0:T(1024)S(1)} %broadcast_clamp_fusion), kind=kCustom, calls=%fused_computation | custom fusion | bytes 12288 | tf_op jit(solution)/shard_map/gather | solution.py:116
  94.1 6.5 %scatter_fusion = f32[131072]{0:T(1024)S(1)} fusion(f32[131072]{0:T(1024)S(1)} %bitcast.667, s32[1024]{0:T(1024)S(1)} %bitcast.718, f32[1024]{0:T(1024)S(1)} %sub.269), kind=kCustom, calls=%fused_computation.1 | custom fusion | flops 1024 | bytes 16384 | tf_op jit(solution)/shard_map/scatter-add | solution.py:117
  100.6 3.0 %add_bitcast_fusion.6 = (f32[1,16,64,128]{3,2,1,0:T(8,128)}, f32[16,64,128]{2,1,0:T(8,128)S(1)}) fusion(f32[16,64,128]{2,1,0:T(8,128)} %get-tuple-element.69, f32[16,64,128]{2,1,0:T(8,128)S(1)} %bitcast.664, f32[16,64,128]{2,1,0:T(8,128)} %get-tuple-element.68, f32[1,13,16,64,128]{4,3,2,1,0:T(8,128)} %param.16), kind=kLoop, calls=%fused_computation.218 | loop fusion | flops 2097152 | bytes 4194304 | tf_op jit(solution)/shard_map/transpose(jvp())/broadcast_in_dim | solution.py:55
  103.6 2.8 %fusion.114 = (f32[16,64,128]{2,1,0:T(8,128)S(1)}, f32[16,64,128]{2,1,0:T(8,128)S(1)}, f32[16,64,128]{2,1,0:T(8,128)S(1)}, f32[16,64,128]{2,1,0:T(8,128)}, f32[1,16,64,128]{3,2,1,0:T(8,128)}) fusion(f32[1,13,16,64,128]{4,3,2,1,0:T(8,128)} %param.16, f32[4,16,64,128]{3,2,1,0:T(8,128)S(1)} %copy_multiply_fusion, f32[16,64,128]{2,1,0:T(8,128)S(1)} %get-tuple-element.52, ...), kind=kLoop, calls=%fused_computation.178 | loop fusion | flops 2228224 | bytes 6291456 | tf_op jit(solution)/shard_map/transpose(jvp())/add_any | solution.py:72
  106.4 0.8 split.152
  107.2 0.9 split.148
  108.1 1.0 split.144
  109.1 1.0 slice_negate_fusion.4
  110.1 0.6 fusion.116
  110.7 0.9 slice_negate_fusion.6
  111.6 0.8 split.150
  112.5 0.8 split.146
  113.3 0.9 slice_negate_fusion.3
  114.2 6.1 %add_bitcast_fusion.7 = (f32[1,16,64,128]{3,2,1,0:T(8,128)}, f32[16,64,128]{2,1,0:T(8,128)S(1)}, f32[16,64,128]{2,1,0:T(8,128)}, f32[16,64,128]{2,1,0:T(8,128)S(...) fusion(f32[16,64,128]{2,1,0:T(8,128)S(1)} %copy-done.15, ...), kind=kLoop, calls=%fused_computation.219 | loop fusion | flops 6160384 | bytes 19742720 | tf_op jit(solution)/shard_map/transpose(jvp())/broadcast_in_dim | solution.py:55
  120.4 0.8 copy-done.23
  121.1 3.0 %add_bitcast_fusion.4 = (f32[1,16,64,128]{3,2,1,0:T(8,128)S(1)}, f32[1,16,64,128]{3,2,1,0:T(8,128)S(1)}, f32[1,16,64,128]{3,2,1,0:T(8,128)S(1)}, f32[1,16,64,128...) fusion(f32[16,64,128]{2,1,0:T(8,128)} %get-tuple-element.43, ...), kind=kLoop, calls=%fused_computation.213 | loop fusion | flops 5111808 | bytes 12537856 | tf_op jit(solution)/shard_map/transpose(jvp())/broadcast_in_dim | solution.py:44
  124.8 1.1 fusion.84
  126.1 0.9 pad_add_fusion
  127.3 0.8 split.176
  128.1 0.9 split.172
  129.0 1.0 split.168
  130.0 1.5 fusion.117
  131.5 1.0 slice_negate_fusion.1
  133.1 0.8 slice_negate_fusion.5
  133.9 0.9 split.170
  134.8 0.9 split.174
  135.6 0.9 slice_negate_fusion
  136.5 1.8 add_bitcast_fusion
  138.4 1.2 fusion.63
  139.6 4.5 %fusion.13 = f32[1,16,64,128]{3,2,1,0:T(8,128)S(1)} fusion(f32[16,64,128]{2,1,0:T(8,128)S(1)} %get-tuple-element.106, f32[13,16,64,128]{3,2,1,0:T(8,128)S(1)} %pad_add_fusion, f32[16,64,128]{2,1,0:T(8,128)S(1)} %get-tuple-element.107, f32[16,64,128]{2,1,0:T(8,128)S(1)} %get-tuple-element.55, f32[15,64,128]{2,1,0:T(8,128)} %slice_negate_fusion.5, ...), kind=kLoop, calls=%fused_computation.21 | loop fusion | flops 6946816 | bytes 16072704 | tf_op jit(solution)/shard_map/transpose(jvp())/broadcast_in_dim | solution.py:55
  144.6 2.6 %copy.52 = f32[4,16,64,128]{3,1,0,2:T(8,128)} copy(f32[4,16,64,128]{3,2,1,0:T(8,128)S(1)} %pad_add_fusion.1) | data formatting | bytes 4194304 | tf_op jit(solution)/shard_map/transpose(jvp())/add_any | solution.py:55
  147.2 60.6 %reduce-scatter.2.cloned.1.call-done = f32[4,16,4,128]{3,1,0,2:T(8,128)} async-done(((f32[4,16,64,128]{3,1,0,2:T(8,128)}), f32[4,16,4,128]{3,1,0,2:T(8,128)}) %reduce-scatter.2.cloned.1.call-update) | async-done | bytes 131088 | tf_op jit(solution)/shard_map/reduce_scatter | solution.py:154
  207.8 1.8 fusion.131
  (158 shorter events, 4.2 us)
Async XLA Ops:
  6.5 9.1 %copy-start.54 = (f32[1,2]{1,0:T(1,128)S(1)}, f32[1,2]{1,0:T(1,128)}, u32[]{:S(2)}) copy-start(f32[1,2]{1,0:T(1,128)} %param.17) | copy-start | bytes 28
  6.5 9.6 %copy-start.52 = (s32[1,1024]{1,0:T(1,128)S(1)}, s32[1,1024]{1,0:T(1,128)}, u32[]{:S(2)}) copy-start(s32[1,1024]{1,0:T(1,128)} %param.19) | copy-start | bytes 12292
  6.5 47.2 %all-gather.2.cloned.1.call-start = ((), (), s32[]{:S(2)}) async-start(), calls=%async_computation.1 | async-start | bytes 2228224 | tf_op jit(solution)/shard_map/all_gather | solution.py:139
  8.2 9.4 %copy-start.53 = (f32[4,4]{1,0:T(4,128)S(1)}, f32[4,4]{1,0:T(4,128)}, u32[]{:S(2)}) copy-start(f32[4,4]{1,0:T(4,128)} %param.23) | copy-start | bytes 196
  8.2 199.6 %reduce-scatter.2.cloned.1.call-start = ((), (), s32[]{:S(2)}) async-start(), calls=%async_computation.2 | async-start | bytes 2228224 | tf_op jit(solution)/shard_map/reduce_scatter | solution.py:154
  53.7 6.9 %slice-start.3 = ((s8[6815744]{0:T(1024)(128)(4,1)}), s8[4194304]{0:T(1024)(128)(4,1)S(1)}, s32[]{:S(2)}) async-start(s8[6815744]{0:T(1024)(128)(4,1)} %bitcast.668), calls=%async_computation.6 | async-start | bytes 8388608
  53.7 6.9 %copy-start.36 = (f32[16,64,128]{2,1,0:T(8,128)S(1)}, f32[16,64,128]{2,1,0:T(8,128)}, u32[]{:S(2)}) copy-start(f32[16,64,128]{2,1,0:T(8,128)} %get-tuple-element.132) | copy-start | bytes 1572868
  53.7 6.9 %copy-start.49 = (f32[15,64,128]{2,1,0:T(8,128)S(1)}, f32[15,64,128]{2,1,0:T(8,128)}, u32[]{:S(2)}) copy-start(f32[15,64,128]{2,1,0:T(8,128)} %get-tuple-element.126) | copy-start | bytes 1474564
  53.7 6.9 %copy-start.50 = (f32[15,64,128]{2,1,0:T(8,128)S(1)}, f32[15,64,128]{2,1,0:T(8,128)}, u32[]{:S(2)}) copy-start(f32[15,64,128]{2,1,0:T(8,128)} %get-tuple-element.127) | copy-start | bytes 1474564
  57.3 3.3 %slice-start.4 = ((s8[6815744]{0:T(1024)(128)(4,1)}), s8[2621440]{0:T(1024)(128)(4,1)S(1)}, s32[]{:S(2)}) async-start(s8[6815744]{0:T(1024)(128)(4,1)} %bitcast.668), calls=%async_computation.7 | async-start | bytes 5242880
  60.5 12.0 %copy-start = (f32[16,64,128]{2,1,0:T(8,128)}, f32[16,64,128]{2,1,0:T(8,128)S(1)}, u32[]{:S(2)}) copy-start(f32[16,64,128]{2,1,0:T(8,128)S(1)} %get-tuple-element.86) | copy-start | bytes 1572868
  60.5 1.3 copy-start.42
  60.5 1.4 copy-start.43
  60.5 1.5 copy-start.46
  61.3 7.3 %copy-start.2 = (f32[16,64,128]{2,1,0:T(8,128)}, f32[16,64,128]{2,1,0:T(8,128)S(1)}, u32[]{:S(2)}) copy-start(f32[16,64,128]{2,1,0:T(8,128)S(1)} %get-tuple-element.92) | copy-start | bytes 1572868
  61.4 2.1 copy-start.25
  63.5 8.2 %copy-start.14 = (f32[16,64,128]{2,1,0:T(8,128)}, f32[16,64,128]{2,1,0:T(8,128)S(1)}, u32[]{:S(2)}) copy-start(f32[16,64,128]{2,1,0:T(8,128)S(1)} %get-tuple-element.122) | copy-start | bytes 1572868
  63.5 9.0 %copy-start.8 = (f32[16,64,128]{2,1,0:T(8,128)}, f32[16,64,128]{2,1,0:T(8,128)S(1)}, u32[]{:S(2)}) copy-start(f32[16,64,128]{2,1,0:T(8,128)S(1)} %get-tuple-element.123) | copy-start | bytes 1572868
  63.5 13.6 %copy-start.10 = (f32[16,64,128]{2,1,0:T(8,128)}, f32[16,64,128]{2,1,0:T(8,128)S(1)}, u32[]{:S(2)}) copy-start(f32[16,64,128]{2,1,0:T(8,128)S(1)} %get-tuple-element.121) | copy-start | bytes 1572868
  64.5 1.8 copy-start.16
  64.5 1.8 copy-start.18
  69.3 8.2 %copy-start.12 = (f32[16,64,128]{2,1,0:T(8,128)}, f32[16,64,128]{2,1,0:T(8,128)S(1)}, u32[]{:S(2)}) copy-start(f32[16,64,128]{2,1,0:T(8,128)S(1)} %get-tuple-element.74) | copy-start | bytes 1572868
  69.3 8.1 %copy-start.27 = (f32[15,64,128]{2,1,0:T(8,128)}, f32[15,64,128]{2,1,0:T(8,128)S(1)}, u32[]{:S(2)}) copy-start(f32[15,64,128]{2,1,0:T(8,128)S(1)} %slice.407) | copy-start | bytes 1474564
  72.5 5.0 %copy-start.4 = (f32[16,64,128]{2,1,0:T(8,128)}, f32[16,64,128]{2,1,0:T(8,128)S(1)}, u32[]{:S(2)}) copy-start(f32[16,64,128]{2,1,0:T(8,128)S(1)} %get-tuple-element.72) | copy-start | bytes 1572868
  73.4 6.0 %copy-start.6 = (f32[16,64,128]{2,1,0:T(8,128)}, f32[16,64,128]{2,1,0:T(8,128)S(1)}, u32[]{:S(2)}) copy-start(f32[16,64,128]{2,1,0:T(8,128)S(1)} %get-tuple-element.70) | copy-start | bytes 1572868
  77.4 16.7 %copy-start.51 = (f32[1,1024]{1,0:T(1,128)S(1)}, f32[1,1024]{1,0:T(1,128)}, u32[]{:S(2)}) copy-start(f32[1,1024]{1,0:T(1,128)} %param.20) | copy-start | bytes 12292
  77.4 16.7 %slice-start.2 = ((f32[1,13,16,64,128]{4,3,2,1,0:T(8,128)}), f32[1,1,16,64,128]{4,3,2,1,0:T(8,128)S(1)}, s32[]{:S(2)}) async-start(f32[1,13,16,64,128]{4,3,2,1,0:T(8,128)} %param.16), calls=%async_computation.5 | async-start | bytes 1048576 | tf_op jit(solution)/shard_map/slice | solution.py:117
  100.6 9.5 %slice-start = ((s8[6815744]{0:T(1024)(128)(4,1)}), s8[4194304]{0:T(1024)(128)(4,1)S(1)}, s32[]{:S(2)}) async-start(s8[6815744]{0:T(1024)(128)(4,1)} %bitcast.662), calls=%async_computation.3 | async-start | bytes 8388608
  103.6 6.5 %slice-start.1 = ((s8[6815744]{0:T(1024)(128)(4,1)}), s8[2621440]{0:T(1024)(128)(4,1)S(1)}, s32[]{:S(2)}) async-start(s8[6815744]{0:T(1024)(128)(4,1)} %bitcast.662), calls=%async_computation.4 | async-start | bytes 5242880
  107.2 7.0 %copy-start.9 = (f32[16,64,128]{2,1,0:T(8,128)S(1)}, f32[16,64,128]{2,1,0:T(8,128)}, u32[]{:S(2)}) copy-start(f32[16,64,128]{2,1,0:T(8,128)} %copy-done.8) | copy-start | bytes 1572868
  107.2 7.0 %copy-start.11 = (f32[16,64,128]{2,1,0:T(8,128)S(1)}, f32[16,64,128]{2,1,0:T(8,128)}, u32[]{:S(2)}) copy-start(f32[16,64,128]{2,1,0:T(8,128)} %copy-done.10) | copy-start | bytes 1572868
  107.2 7.0 %copy-start.15 = (f32[16,64,128]{2,1,0:T(8,128)S(1)}, f32[16,64,128]{2,1,0:T(8,128)}, u32[]{:S(2)}) copy-start(f32[16,64,128]{2,1,0:T(8,128)} %copy-done.14) | copy-start | bytes 1572868
  110.7 3.5 %copy-start.24 = (f32[16,64,128]{2,1,0:T(8,128)}, f32[16,64,128]{2,1,0:T(8,128)S(1)}, u32[]{:S(2)}) copy-start(f32[16,64,128]{2,1,0:T(8,128)S(1)} %get-tuple-element.97) | copy-start | bytes 1572868
  120.3 0.8 copy-start.23
  124.7 1.2 copy-start.20
  124.7 1.2 copy-start.21
  124.7 1.3 copy-start.22
  126.1 3.9 %copy-start.17 = (f32[16,64,128]{2,1,0:T(8,128)S(1)}, f32[16,64,128]{2,1,0:T(8,128)}, u32[]{:S(2)}) copy-start(f32[16,64,128]{2,1,0:T(8,128)} %copy-done.16) | copy-start | bytes 1572868
  126.1 3.9 %copy-start.19 = (f32[16,64,128]{2,1,0:T(8,128)S(1)}, f32[16,64,128]{2,1,0:T(8,128)}, u32[]{:S(2)}) copy-start(f32[16,64,128]{2,1,0:T(8,128)} %copy-done.18) | copy-start | bytes 1572868
  131.5 5.0 %copy-start.1 = (f32[16,64,128]{2,1,0:T(8,128)S(1)}, f32[16,64,128]{2,1,0:T(8,128)}, u32[]{:S(2)}) copy-start(f32[16,64,128]{2,1,0:T(8,128)} %copy-done) | copy-start | bytes 1572868
  131.5 5.0 %copy-start.3 = (f32[16,64,128]{2,1,0:T(8,128)S(1)}, f32[16,64,128]{2,1,0:T(8,128)}, u32[]{:S(2)}) copy-start(f32[16,64,128]{2,1,0:T(8,128)} %copy-done.2) | copy-start | bytes 1572868
  131.5 5.0 %copy-start.26 = (f32[15,64,128]{2,1,0:T(8,128)S(1)}, f32[15,64,128]{2,1,0:T(8,128)}, u32[]{:S(2)}) copy-start(f32[15,64,128]{2,1,0:T(8,128)} %copy-done.25) | copy-start | bytes 1474564
  131.5 5.0 %copy-start.29 = (f32[16,64,128]{2,1,0:T(8,128)S(1)}, f32[16,64,128]{2,1,0:T(8,128)}, u32[]{:S(2)}) copy-start(f32[16,64,128]{2,1,0:T(8,128)} %get-tuple-element.81) | copy-start | bytes 1572868
  131.5 5.0 %copy-start.30 = (f32[16,64,128]{2,1,0:T(8,128)S(1)}, f32[16,64,128]{2,1,0:T(8,128)}, u32[]{:S(2)}) copy-start(f32[16,64,128]{2,1,0:T(8,128)} %get-tuple-element.100) | copy-start | bytes 1572868
  131.5 5.0 %copy-start.31 = (f32[16,64,128]{2,1,0:T(8,128)S(1)}, f32[16,64,128]{2,1,0:T(8,128)}, u32[]{:S(2)}) copy-start(f32[16,64,128]{2,1,0:T(8,128)} %get-tuple-element.102) | copy-start | bytes 1572868
  133.0 5.3 %copy-start.5 = (f32[16,64,128]{2,1,0:T(8,128)S(1)}, f32[16,64,128]{2,1,0:T(8,128)}, u32[]{:S(2)}) copy-start(f32[16,64,128]{2,1,0:T(8,128)} %copy-done.4) | copy-start | bytes 1572868
  133.0 5.3 %copy-start.7 = (f32[16,64,128]{2,1,0:T(8,128)S(1)}, f32[16,64,128]{2,1,0:T(8,128)}, u32[]{:S(2)}) copy-start(f32[16,64,128]{2,1,0:T(8,128)} %copy-done.6) | copy-start | bytes 1572868
  133.0 5.3 %copy-start.13 = (f32[16,64,128]{2,1,0:T(8,128)S(1)}, f32[16,64,128]{2,1,0:T(8,128)}, u32[]{:S(2)}) copy-start(f32[16,64,128]{2,1,0:T(8,128)} %copy-done.12) | copy-start | bytes 1572868
  133.0 5.3 %copy-start.28 = (f32[15,64,128]{2,1,0:T(8,128)S(1)}, f32[15,64,128]{2,1,0:T(8,128)}, u32[]{:S(2)}) copy-start(f32[15,64,128]{2,1,0:T(8,128)} %copy-done.27) | copy-start | bytes 1474564
  133.0 5.3 %copy-start.38 = (f32[16,63,128]{2,1,0:T(8,128)S(1)}, f32[16,63,128]{2,1,0:T(8,128)}, u32[]{:S(2)}) copy-start(f32[16,63,128]{2,1,0:T(8,128)} %slice.427) | copy-start | bytes 1548292
  133.0 5.3 %copy-start.39 = (f32[16,64,127]{2,1,0:T(8,128)S(1)}, f32[16,64,127]{2,1,0:T(8,128)}, u32[]{:S(2)}) copy-start(f32[16,64,127]{2,1,0:T(8,128)} %slice.425) | copy-start | bytes 1560580
  133.0 5.3 %copy-start.40 = (f32[16,63,128]{2,1,0:T(8,128)S(1)}, f32[16,63,128]{2,1,0:T(8,128)}, u32[]{:S(2)}) copy-start(f32[16,63,128]{2,1,0:T(8,128)} %slice.424) | copy-start | bytes 1548292
  133.0 5.3 %copy-start.41 = (f32[16,64,127]{2,1,0:T(8,128)S(1)}, f32[16,64,127]{2,1,0:T(8,128)}, u32[]{:S(2)}) copy-start(f32[16,64,127]{2,1,0:T(8,128)} %slice.423) | copy-start | bytes 1560580
  133.0 5.3 %copy-start.47 = (f32[15,64,128]{2,1,0:T(8,128)S(1)}, f32[15,64,128]{2,1,0:T(8,128)}, u32[]{:S(2)}) copy-start(f32[15,64,128]{2,1,0:T(8,128)} %slice.426) | copy-start | bytes 1474564
  133.1 5.3 %copy-start.48 = (f32[15,64,128]{2,1,0:T(8,128)S(1)}, f32[15,64,128]{2,1,0:T(8,128)}, u32[]{:S(2)}) copy-start(f32[15,64,128]{2,1,0:T(8,128)} %slice.428) | copy-start | bytes 1474564
  138.4 1.2 copy-start.44
  139.5 4.6 %copy-start.32 = (f32[1,16,64,128]{3,2,1,0:T(8,128)S(1)}, f32[1,16,64,128]{3,2,1,0:T(8,128)}, u32[]{:S(2)}) copy-start(f32[1,16,64,128]{3,2,1,0:T(8,128)} %get-tuple-element.149) | copy-start | bytes 1572868
  139.6 4.6 %copy-start.33 = (f32[1,16,64,128]{3,2,1,0:T(8,128)S(1)}, f32[1,16,64,128]{3,2,1,0:T(8,128)}, u32[]{:S(2)}) copy-start(f32[1,16,64,128]{3,2,1,0:T(8,128)} %get-tuple-element.41) | copy-start | bytes 1572868
  139.6 4.6 %copy-start.34 = (f32[1,16,64,128]{3,2,1,0:T(8,128)S(1)}, f32[1,16,64,128]{3,2,1,0:T(8,128)}, u32[]{:S(2)}) copy-start(f32[1,16,64,128]{3,2,1,0:T(8,128)} %get-tuple-element.114) | copy-start | bytes 1572868
  139.6 4.6 %copy-start.35 = (f32[1,16,64,128]{3,2,1,0:T(8,128)S(1)}, f32[1,16,64,128]{3,2,1,0:T(8,128)}, u32[]{:S(2)}) copy-start(f32[1,16,64,128]{3,2,1,0:T(8,128)} %get-tuple-element.148) | copy-start | bytes 1572868
  139.6 4.6 %copy-start.37 = (f32[1,16,64,128]{3,2,1,0:T(8,128)S(1)}, f32[1,16,64,128]{3,2,1,0:T(8,128)}, u32[]{:S(2)}) copy-start(f32[1,16,64,128]{3,2,1,0:T(8,128)} %add_bitcast_fusion) | copy-start | bytes 1572868
  139.6 4.6 %copy-start.45 = (f32[1,16,64,128]{3,2,1,0:T(8,128)S(1)}, f32[1,16,64,128]{3,2,1,0:T(8,128)}, u32[]{:S(2)}) copy-start(f32[1,16,64,128]{3,2,1,0:T(8,128)} %get-tuple-element.51) | copy-start | bytes 1572868
Sparse Core Ops, SparseCore 0:
  9.5 44.1 all-gather.1
  147.3 60.4 reduce-scatter.1
where the time goes:
time: 217 us; the launch traced here: 216 us
  waiting for transfers between devices  91.9 us (42%)
  other arithmetic  64.5 us (30%)
  local copies, waits for them, and re-layouts  45 us (21%)
  between operations  15 us (7%)
    reduce_scatter x1, waiting for transfers between devices, per_device(): summed = lax.psum_scatter(total, 'shot', scatter_dimension=2, tiled=True)  60.6 us
    all_gather x1, waiting for transfers between devices, per_device(): whole_model = lax.all_gather(material, 'shot', axis=2, tiled=True)  31.2 us
    gather x1, local copies, waits for them, and re-layouts, shot_gradient(): misfit = final[12].reshape(-1)[receivers] - observed  12.6 us
    broadcast_in_dim x2, other arithmetic, advance(): model[3]  10.7 us
    slice x22, local copies, waits for them, and re-layouts, forward_diff(): lax.slice_in_dim(field, 1, count, axis=axis)  10.6 us
    scatter-add x1, other arithmetic, shot_gradient(): adjoint[12].reshape(-1).at[receivers].add(misfit).reshape(adjoint[12].shape)  6.5 us
    split x12, local copies, waits for them, and re-layouts, backward_diff(): jnp.concatenate([jnp.zeros_like(lax.slice_in_dim(field, 0, 1, axis=axis))...  6.01 us
    neg x7, other arithmetic, backward_diff(): return field - behind  5.78 us
  transfers between devices with their start and end apart: 2, of which 2 were waited for; matrix products, arithmetic and copies ran while one was open for 6% of the time, Pallas kernels for 0%

commit v1 on v0

v1 whole, which is shorter than its diff:
```python
import functools

import jax
import jax.numpy as jnp
from jax import lax
from jax.experimental import pallas as pl
from jax.experimental.pallas import tpu as pltpu
from jax.sharding import PartitionSpec as P

BIOT_COEFF = 0.8
RHO_BULK = 2.2
RHO_FLUID = 1.0
MASS_FLUID = 2.5
TIME_STEP = 0.25
DET = RHO_BULK * MASS_FLUID - RHO_FLUID * RHO_FLUID
C_M = TIME_STEP * MASS_FLUID / DET
C_A = TIME_STEP * RHO_BULK / DET
C_B = TIME_STEP * RHO_FLUID / DET

VX, VZ, VY, QX, QZ, QY, SXX, SZZ, SYY, SXZ, SXY, SZY, PR = range(13)
MESH = pl.DeviceIdType.MESH
F32 = jnp.float32


def coordinates(n):
    me = lax.axis_index("shot")
    return me, lax.rem(me, 2), lax.rem(me // 2, 2), me // 4, n // 4


def index_of(z, y, core):
    return (z * 2 + y) * 2 + core


def greet(n):
    me, core, y, z, zs = coordinates(n)
    barrier = pltpu.get_barrier_semaphore()
    peers = [index_of(z, y, 1 - core), index_of(z, 1 - y, core)]
    peers += [index_of(lax.rem(z + d, zs), y, core) for d in range(1, zs)]
    for peer in peers:
        pl.semaphore_signal(barrier, inc=1, device_id={"shot": peer}, device_id_type=MESH)
    pl.semaphore_wait(barrier, len(peers))


def gather_kernel(n, own_ref, out_ref, local_sem, zs_sem, zr_sem, ys_sem, yr_sem, cs_sem, cr_sem):
    me, core, y, z, zs = coordinates(n)
    other_core = {"shot": index_of(z, y, 1 - core)}
    other_side = {"shot": index_of(z, 1 - y, core)}
    mine = pltpu.make_async_copy(own_ref, out_ref.at[me], local_sem)
    mine.start()
    greet(n)

    def send(src, slot, send_sem, recv_sem, target):
        copy = pltpu.make_async_remote_copy(
            src_ref=src, dst_ref=out_ref.at[slot], send_sem=send_sem, recv_sem=recv_sem,
            device_id=target, device_id_type=MESH)
        copy.start()
        return copy

    along, across, inside = [], [], []
    across.append(send(own_ref, me, ys_sem.at[0], yr_sem.at[0], other_side))
    for d in range(1, zs):
        target = {"shot": index_of(lax.rem(z + d, zs), y, core)}
        along.append(send(own_ref, me, zs_sem.at[d], zr_sem.at[d], target))
    inside.append(send(own_ref, me, cs_sem.at[0], cr_sem.at[0], other_core))
    for d in range(1, zs):
        along[d - 1].wait_recv()
        slot = index_of(lax.rem(z + zs - d, zs), y, core)
        across.append(send(out_ref.at[slot], slot, ys_sem.at[d], yr_sem.at[d], other_side))
        inside.append(send(out_ref.at[slot], slot, cs_sem.at[d], cr_sem.at[d], other_core))
    for d in range(zs):
        across[d].wait_recv()
        slot = index_of(lax.rem(z + zs - d, zs), 1 - y, core)
        inside.append(send(out_ref.at[slot], slot, cs_sem.at[zs + d], cr_sem.at[zs + d], other_core))
    for copy in inside:
        copy.wait_recv()
    for copy in along + across + inside:
        copy.wait_send()
    mine.wait()


def gather_slabs(own, n):
    zs = n // 4
    dma = pltpu.SemaphoreType.DMA
    return pl.pallas_call(
        functools.partial(gather_kernel, n),
        out_shape=jax.ShapeDtypeStruct((n,) + own.shape, own.dtype),
        in_specs=[pl.BlockSpec(memory_space=pltpu.VMEM)],
        out_specs=pl.BlockSpec(memory_space=pltpu.VMEM),
        scratch_shapes=[dma, dma((zs,)), dma((zs,)), dma((zs,)), dma((zs,)), dma((2 * zs,)), dma((2 * zs,))],
        compiler_params=pltpu.CompilerParams(collective_id=0, has_side_effects=True, vmem_limit_bytes=8 << 20),
        name="gather_slabs",
    )(own)


def scatter_kernel(n, term_ref, out_ref, from_core, to_side, from_side, to_line, from_line,
                   cs_sem, cr_sem, ys_sem, yr_sem, zs_sem, zr_sem):
    me, core, y, z, zs = coordinates(n)
    other_core = {"shot": index_of(z, y, 1 - core)}
    other_side = {"shot": index_of(z, 1 - y, core)}
    greet(n)

    def send(src, dst, send_sem, recv_sem, target):
        copy = pltpu.make_async_remote_copy(
            src_ref=src, dst_ref=dst, send_sem=send_sem, recv_sem=recv_sem,
            device_id=target, device_id_type=MESH)
        copy.start()
        return copy

    order = list(range(1, zs)) + [0]
    place = {d: lax.rem(z + d, zs) for d in order}
    inside, across, along = {}, {}, {}
    for far in (1, 0):
        side = 1 - y if far else y
        for d in order:
            k = far * zs + d
            inside[k] = send(term_ref.at[index_of(place[d], side, 1 - core)], from_core.at[k],
                             cs_sem.at[k], cr_sem.at[k], other_core)
    for d in order:
        inside[zs + d].wait_recv()
        to_side[d] = term_ref[index_of(place[d], 1 - y, core)] + from_core[zs + d]
        across[d] = send(to_side.at[d], from_side.at[d], ys_sem.at[d], yr_sem.at[d], other_side)
    for d in order:
        inside[d].wait_recv()
        across[d].wait_recv()
        total = term_ref[index_of(place[d], y, core)] + from_core[d] + from_side[d]
        to_line[d] = total
        if d:
            target = {"shot": index_of(place[d], y, core)}
            along[d] = send(to_line.at[d], from_line.at[d], zs_sem.at[d], zr_sem.at[d], target)
    result = to_line[0]
    for d in range(1, zs):
        along[d].wait_recv()
        result = result + from_line[d]
    out_ref[...] = result
    for copies in (inside, across, along):
        for copy in copies.values():
            copy.wait_send()


def scatter_slabs(terms):
    n, slab = terms.shape[0], terms.shape[1:]
    zs = n // 4
    dma = pltpu.SemaphoreType.DMA
    return pl.pallas_call(
        functools.partial(scatter_kernel, n),
        out_shape=jax.ShapeDtypeStruct(slab, terms.dtype),
        in_specs=[pl.BlockSpec(memory_space=pltpu.VMEM)],
        out_specs=pl.BlockSpec(memory_space=pltpu.VMEM),
        scratch_shapes=[
            pltpu.VMEM((2 * zs,) + slab, F32),
            pltpu.VMEM((zs,) + slab, F32), pltpu.VMEM((zs,) + slab, F32),
            pltpu.VMEM((zs,) + slab, F32), pltpu.VMEM((zs,) + slab, F32),
            dma((2 * zs,)), dma((2 * zs,)), dma((zs,)), dma((zs,)), dma((zs,)), dma((zs,))],
        compiler_params=pltpu.CompilerParams(collective_id=1, has_side_effects=True, vmem_limit_bytes=16 << 20),
        name="scatter_slabs",
    )(terms)


class Window:
    def __init__(self, x, z0, zc, nz, ny):
        self.x, self.z0, self.zc, self.nz = x, z0, zc, nz
        self.row = lax.broadcasted_iota(jnp.int32, (zc, ny), 0)
        self.lane = lax.broadcasted_iota(jnp.int32, (zc, ny), 1)
        self.ny = ny
        self.seen = {}

    def at(self, ref, f, dx=0, dz=0):
        key = (id(ref), f, dx, dz)
        if key in self.seen:
            return self.seen[key]
        plane = self.x + 1 + dx
        lo = self.z0 + dz
        if lo < 0:
            value = self.at(ref, f, dx)
            value = jnp.where(self.row == 0, 0.0, pltpu.roll(value, 1, 0))
        elif lo + self.zc > self.nz:
            value = self.at(ref, f, dx)
            value = jnp.where(self.row == self.zc - 1, 0.0, pltpu.roll(value, self.zc - 1, 0))
        else:
            value = ref[f, plane, lo:lo + self.zc, :]
        self.seen[key] = value
        return value

    def fx(self, ref, f):
        return self.at(ref, f, 1) - self.at(ref, f)

    def bx(self, ref, f):
        return self.at(ref, f) - self.at(ref, f, -1)

    def fz(self, ref, f):
        return self.at(ref, f, 0, 1) - self.at(ref, f)

    def bz(self, ref, f):
        return self.at(ref, f) - self.at(ref, f, 0, -1)

    def fy(self, ref, f):
        value = self.at(ref, f)
        return jnp.where(self.lane == self.ny - 1, 0.0, pltpu.roll(value, self.ny - 1, 1)) - value

    def by(self, ref, f):
        value = self.at(ref, f)
        return value - jnp.where(self.lane == 0, 0.0, pltpu.roll(value, 1, 1))

    def put(self, ref, f, value):
        ref[f, self.x + 1, self.z0:self.z0 + self.zc, :] = value


def shot_kernel(n, zc, fwd_hbm, adj_hbm, amp_ref, src_ref, rec_ref, obs_ref, gathered_ref, class_ref, cf_ref,
                out_ref, st, ad, q1, q2, e1, be, bf, mat, grad, cnt, obs, fwd_sem, adj_sem):
    planes, nz, ny = class_ref.shape
    piece = gathered_ref.shape[2]
    classes = cf_ref.shape[1]

    def fwd_copy(x):
        return pltpu.make_async_copy(fwd_hbm.at[:, x], st.at[:, x + 1], fwd_sem.at[x])

    def adj_copy(x):
        return pltpu.make_async_copy(adj_hbm.at[:, x], ad.at[:, x + 1], adj_sem.at[x])

    for x in range(planes):
        fwd_copy(x).start()
    for x in range(planes):
        adj_copy(x).start()

    zero_plane = jnp.zeros((nz, ny), F32)
    for ref in (st, q1, q2, be, bf):
        for f in range(ref.shape[0]):
            ref[f, 0] = zero_plane
            ref[f, planes + 1] = zero_plane

    cells = rec_ref[...]
    rows = lax.div(cells, jnp.int32(ny))
    lanes = cells - rows * ny
    count = cells.shape[1]
    value = obs_ref[...]
    hi = value.astype(jnp.bfloat16).astype(F32)
    mid = (value - hi).astype(jnp.bfloat16).astype(F32)
    low = value - hi - mid
    hit = lax.broadcasted_iota(jnp.int32, (ny, count), 0) == lanes
    columns = jnp.concatenate(
        [jnp.where(hit, part, 0.0).astype(jnp.bfloat16) for part in (jnp.ones_like(value), hi, mid, low)], axis=0)

    def place_receivers(x, carry):
        at_row = lax.broadcasted_iota(jnp.int32, (nz, count), 0) + x * nz == rows
        product = lax.dot_general(
            jnp.where(at_row, 1.0, 0.0).astype(jnp.bfloat16), columns, (((1,), (1,)), ((), ())),
            preferred_element_type=F32)
        cnt[x] = product[:, :ny]
        obs[x] = product[:, ny:2 * ny] + product[:, 2 * ny:3 * ny] + product[:, 3 * ny:]
        return carry

    lax.fori_loop(0, planes, place_receivers, 0)

    def factor_of(k, cls):
        factor = jnp.full(cls.shape, cf_ref[k, classes - 1], F32)
        for c in range(classes - 1):
            factor = jnp.where(cls == c, cf_ref[k, c], factor)
        return factor

    scales = (TIME_STEP, 2.0 * TIME_STEP, TIME_STEP, 1.0)

    def build_model(x, carry):
        cls = class_ref[x]
        for k in range(4):
            for d in range(n):
                mat[k, x + 1, d * piece:(d + 1) * piece, :] = gathered_ref[d, k * planes + x]
            mat[k, x + 1] = mat[k, x + 1] * factor_of(k, cls) * scales[k]
        return carry

    lax.fori_loop(0, planes, build_model, 0)

    source = src_ref[0]
    L, U, B, D = range(4)

    def sweep(body, before=None):
        def plane(x, carry):
            if before is not None:
                before(x)
            for z0 in range(0, nz, zc):
                body(Window(x, z0, zc, nz, ny))
            return carry
        lax.fori_loop(0, planes, plane, 0)

    def velocities(q_old, base, q_new, w):
        damp = w.at(mat, D)
        forces = (
            w.fx(st, SXX) + w.bz(st, SXZ) + w.by(st, SXY),
            w.bx(st, SXZ) + w.fz(st, SZZ) + w.by(st, SZY),
            w.bx(st, SXY) + w.bz(st, SZY) + w.fy(st, SYY))
        slopes = (w.fx(st, PR), w.fz(st, PR), w.fy(st, PR))
        for i in range(3):
            flux = w.at(q_old, base + i)
            pull = slopes[i] + damp * flux
            w.put(st, VX + i, w.at(st, VX + i) + (C_M * forces[i] + C_B * pull))
            w.put(q_new, i, flux - (C_A * pull + C_B * forces[i]))

    def strains(q, w):
        exx, ezz, eyy = w.bx(st, VX), w.bz(st, VZ), w.by(st, VY)
        dv = exx + ezz + eyy
        g = BIOT_COEFF * dv + (w.bx(q, 0) + w.bz(q, 1) + w.by(q, 2))
        gxz = w.fz(st, VX) + w.fx(st, VZ)
        gxy = w.fy(st, VX) + w.fx(st, VY)
        gzy = w.fy(st, VZ) + w.fz(st, VY)
        return exx, ezz, eyy, gxz, gxy, gzy, dv, g

    def add_source(w, section, pressure):
        here = (w.row + (w.x * nz + w.z0)) * ny + w.lane == source
        return pressure + jnp.where(here, amp_ref[0, section], 0.0)

    def correlate(w, bars, bar_p, terms):
        exx, ezz, eyy, gxz, gxy, gzy, dv, g = terms
        trace = bars[0] + bars[1] + bars[2]
        aside = BIOT_COEFF * trace - bar_p
        g_lame = trace * dv
        g_shear = 2.0 * (bars[0] * exx + bars[1] * ezz + bars[2] * eyy) + (
            bars[3] * gxz + bars[4] * gxy + bars[5] * gzy)
        g_biot = g * aside
        h = w.at(mat, B) * aside
        common = w.at(mat, L) * trace + BIOT_COEFF * h
        shear2 = w.at(mat, U)
        shear1 = 0.5 * shear2
        for i in range(3):
            w.put(be, i, shear2 * bars[i] + common)
            w.put(be, 3 + i, shear1 * bars[3 + i])
        w.put(be, 6, h)
        return g_lame, g_shear, g_biot

    def bar_motion(w):
        vels = (
            w.at(ad, VX) - (w.fx(be, 0) + w.bz(be, 3) + w.by(be, 4)),
            w.at(ad, VZ) - (w.fz(be, 1) + w.bx(be, 3) + w.by(be, 5)),
            w.at(ad, VY) - (w.fy(be, 2) + w.bx(be, 4) + w.bz(be, 5)))
        fluxes = (
            w.at(ad, QX) - w.fx(be, 6), w.at(ad, QZ) - w.fz(be, 6), w.at(ad, QY) - w.fy(be, 6))
        return vels, fluxes

    def rows_of(ref, k, w):
        return ref[k, w.x, w.z0:w.z0 + zc, :]

    fwd_copy(0).wait()

    def next_forward(x):
        @pl.when(x + 1 < planes)
        def _():
            fwd_copy(x + 1).wait()

    sweep(functools.partial(velocities, st, QX, q1), next_forward)

    def stresses(w):
        terms = strains(q1, w)
        exx, ezz, eyy, gxz, gxy, gzy, dv, g = terms
        bg = w.at(mat, B) * g
        bulk = w.at(mat, L) * dv + BIOT_COEFF * bg
        shear2 = w.at(mat, U)
        shear1 = 0.5 * shear2
        for i, e in enumerate((exx, ezz, eyy)):
            w.put(st, SXX + i, w.at(st, SXX + i) + (shear2 * e + bulk))
        for i, e in enumerate((gxz, gxy, gzy)):
            w.put(st, SXZ + i, w.at(st, SXZ + i) + shear1 * e)
        w.put(st, PR, add_source(w, 0, w.at(st, PR) - bg))
        for i, e in enumerate((exx, ezz, eyy, gxz, gxy, gzy, g)):
            e1[i, w.x, w.z0:w.z0 + zc, :] = e

    sweep(stresses)

    sweep(functools.partial(velocities, q1, 0, q2))

    def turn(w):
        terms = strains(q2, w)
        final = add_source(w, 1, w.at(st, PR) - w.at(mat, B) * terms[7])
        here = slice(w.z0, w.z0 + zc)
        bar_p = w.at(ad, PR) + (cnt[w.x, here, :] * final - obs[w.x, here, :])
        w.put(ad, PR, bar_p)
        parts = correlate(w, [w.at(ad, SXX + i) for i in range(6)], bar_p, terms)
        for k in range(3):
            grad[k, w.x, here, :] = parts[k]

    sweep(turn, lambda x: adj_copy(x).wait())

    def back_motion(w):
        vels, fluxes = bar_motion(w)
        damp = w.at(mat, D)
        total = None
        for i in range(3):
            bar_f = C_M * vels[i] - C_B * fluxes[i]
            bar_r = C_A * fluxes[i] - C_B * vels[i]
            w.put(bf, i, bar_f)
            w.put(bf, 3 + i, bar_r)
            part = w.at(q1, i) * bar_r
            total = part if total is None else total + part
            w.put(ad, VX + i, vels[i])
            w.put(ad, QX + i, fluxes[i] - damp * bar_r)
        grad[3, w.x, w.z0:w.z0 + zc, :] = total

    sweep(back_motion)

    def back_stress(w):
        bars = (
            w.at(ad, SXX) - w.bx(bf, 0),
            w.at(ad, SZZ) - w.bz(bf, 1),
            w.at(ad, SYY) - w.by(bf, 2),
            w.at(ad, SXZ) - (w.fz(bf, 0) + w.fx(bf, 1)),
            w.at(ad, SXY) - (w.fy(bf, 0) + w.fx(bf, 2)),
            w.at(ad, SZY) - (w.fy(bf, 1) + w.fz(bf, 2)))
        bar_p = w.at(ad, PR) + (w.bx(bf, 3) + w.bz(bf, 4) + w.by(bf, 5))
        terms = [rows_of(e1, i, w) for i in range(6)]
        terms += [terms[0] + terms[1] + terms[2], rows_of(e1, 6, w)]
        parts = correlate(w, bars, bar_p, terms)
        for k in range(3):
            grad[k, w.x, w.z0:w.z0 + zc, :] = rows_of(grad, k, w) + parts[k]

    sweep(back_stress)

    root = float(n) ** 0.5
    signs = (TIME_STEP / root, TIME_STEP / root, TIME_STEP / root, -1.0 / root)

    def finish(w):
        vels, fluxes = bar_motion(w)
        damp = rows_of(grad, 3, w)
        for i in range(3):
            damp = damp + w.at(st, QX + i) * (C_A * fluxes[i] - C_B * vels[i])
        cls = class_ref[w.x, w.z0:w.z0 + zc, :]
        for k in range(4):
            total = damp if k == 3 else rows_of(grad, k, w)
            total = total * (factor_of(k, cls) * signs[k])
            for r in range(0, zc, piece):
                out_ref[(w.z0 + r) // piece, k * planes + w.x] = total[r:r + piece]

    sweep(finish)


def shot_terms(forward, adjoint, amplitudes, source, receivers, observed, gathered, cell_class, class_factors, n):
    fields, planes, nz, ny = forward.shape
    vmem = pl.BlockSpec(memory_space=pltpu.VMEM)
    smem = pl.BlockSpec(memory_space=pltpu.SMEM)
    hbm = pl.BlockSpec(memory_space=pl.ANY)
    padded = lambda f: pltpu.VMEM((f, planes + 2, nz, ny), F32)
    plain = lambda f: pltpu.VMEM((f, planes, nz, ny), F32)
    return pl.pallas_call(
        functools.partial(shot_kernel, n, 8),
        out_shape=jax.ShapeDtypeStruct(gathered.shape, F32),
        in_specs=[hbm, hbm, smem, smem, vmem, vmem, vmem, vmem, smem],
        out_specs=vmem,
        scratch_shapes=[
            padded(fields), padded(fields), padded(3), padded(3), plain(7), padded(7), padded(6), padded(4), plain(4),
            pltpu.VMEM((planes, nz, ny), F32), pltpu.VMEM((planes, nz, ny), F32),
            pltpu.SemaphoreType.DMA((planes,)), pltpu.SemaphoreType.DMA((planes,))],
        compiler_params=pltpu.CompilerParams(vmem_limit_bytes=48 << 20),
        name="shot_terms",
    )(forward, adjoint, amplitudes, source, receivers, observed, gathered, cell_class, class_factors)


def per_device(forward_state, adjoint_state, source_amp, source_cell, receiver_cells, recorded, material,
               cell_class, class_factors):
    n = lax.axis_size("shot")
    params, planes, piece, ny = material.shape
    gathered = gather_slabs(material.reshape(params * planes, piece, ny), n)
    terms = shot_terms(forward_state[0], adjoint_state[0], source_amp, source_cell, receiver_cells, recorded,
                       gathered, cell_class, class_factors, n)
    return scatter_slabs(terms).reshape(material.shape)


def solution(mesh):
    placed = (
        P(("groups", "shot"), None, None, None, None),
        P(("groups", "shot"), None, None, None, None),
        P(("groups", "shot"), None),
        P(("groups", "shot")),
        P(("groups", "shot"), None),
        P(("groups", "shot"), None),
        P(None, "groups", "shot", None),
        P("groups", None, None),
        P(),
    )
    return jax.shard_map(
        per_device, mesh=mesh, in_specs=placed, out_specs=P(None, "groups", "shot", None), check_vma=False)
```

time: 217 us -> 74.9 us (0.35)
  waiting for transfers between devices: 91.9 us -> 0 us
  Pallas kernels: 0 us -> 68.6 us
  other arithmetic: 64.5 us -> 0 us
  local copies, waits for them, and re-layouts: 45 us -> 5.3 us
  between operations: 15 us -> 0.7 us
    pallas_call x0 -> x3, Pallas kernels: none -> 68.6 us  [the longest x1 23.6 us: gather_slabs(): pl.pallas_call(functools.partial(gather_kernel, n), out_shape=jax.ShapeDt...]
    reduce_scatter x1 -> x0, waiting for transfers between devices: 60.6 us -> none  [per_device(): summed = lax.psum_scatter(total, 'shot', scatter_dimension=2, tiled=True)]
    all_gather x1 -> x0, waiting for transfers between devices: 31.2 us -> none  [per_device(): whole_model = lax.all_gather(material, 'shot', axis=2, tiled=True)]
    broadcast_in_dim x7 -> x0, other arithmetic: 20.7 us -> none  [the longest x2 10.7 us: advance(): model[3]]
    slice x32 -> x0, local copies, waits for them, and re-layouts: 14.3 us -> none  [the longest x22 10.6 us: forward_diff(): lax.slice_in_dim(field, 1, count, axis=axis)]
    gather x1 -> x0, local copies, waits for them, and re-layouts: 12.6 us -> none  [shot_gradient(): misfit = final[12].reshape(-1)[receivers] - observed]
    add x11 -> x0, other arithmetic: 11.3 us -> none  [the longest x2 3.96 us: advance(): vel_y + TIME_STEP * (MASS_FLUID * force_y - RHO_FLUID * drag_y) / determi...]
    scatter-add x3 -> x0, other arithmetic: 9.46 us -> none  [the longest x1 6.5 us: shot_gradient(): adjoint[12].reshape(-1).at[receivers].add(misfit).reshape(adjoint[12].shape)]
  transfers between devices with their start and end apart: 2 -> 0, of which waited for: 2 -> 0; matrix products, arithmetic and copies ran while one was open for 6% -> 0% of each run, Pallas kernels for 0% -> 0%
where the time goes in v1:
time: 74.9 us; the launch traced here: 74.6 us
  Pallas kernels  68.6 us (92%)
  local copies, waits for them, and re-layouts  5.3 us (7%)
    pallas_call x1, Pallas kernels, gather_slabs(): pl.pallas_call(functools.partial(gather_kernel, n), out_shape=jax.ShapeDt...  23.6 us
    pallas_call x1, Pallas kernels, scatter_slabs(): pl.pallas_call(functools.partial(scatter_kernel, n), out_shape=jax.ShapeD...  22.8 us
    pallas_call x1, Pallas kernels, shot_terms(): pl.pallas_call(functools.partial(shot_kernel, n, 8), out_shape=jax.ShapeD...  22.2 us
    unnamed x13, local copies, waits for them, and re-layouts  5.3 us

profile of v1, /device:TPU:0, one launch (start us, length us, event | category | flops | bytes accessed | tf_op | source)
XLA Modules:
  0.0 74.6 jit_solution(6495922359261390397)
XLA Ops:
  0.7 0.0 copy-start.1
  0.7 0.9 %copy-done.1 = f32[4,16,4,128]{3,2,1,0:T(4,128)S(1)} copy-done((f32[4,16,4,128]{3,2,1,0:T(4,128)S(1)}, f32[4,16,4,128]{3,2,1,0:T(4,128)}, u32[]{:S(2)}) %copy-start.1) | copy-done | bytes 131096
  1.6 23.6 %gather_slabs.1.gathered_ref = f32[16,64,4,128]{3,2,1,0:T(4,128)S(1)} custom-call(f32[64,4,128]{2,1,0:T(4,128)S(1)} %bitcast.5), custom_call_target="tpu_custom_call" | custom-call | tf_op jit(solution)/shard_map/gather_slabs/pallas_call | solution.py:84
  25.2 0.0 copy-start
  25.2 1.0 %copy-done = s32[16,64,128]{2,1,0:T(8,128)S(1)} copy-done((s32[16,64,128]{2,1,0:T(8,128)S(1)}, s32[16,64,128]{2,1,0:T(8,128)}, u32[]{:S(2)}) %copy-start) | copy-done | bytes 524312
  26.2 0.0 copy-start.2
  26.2 0.7 copy-done.2
  26.9 0.0 copy-start.3
  26.9 0.7 copy-done.3
  27.6 0.0 copy-start.4
  27.6 0.7 copy-done.4
  28.3 0.0 copy-start.5
  28.3 0.7 copy-done.5
  28.9 22.2 %shot_terms.1.term_ref = f32[16,64,4,128]{3,2,1,0:T(4,128)S(1)} custom-call(f32[13,16,64,128]{3,2,1,0:T(8,128)} %bitcast.6, f32[13,16,64,128]{3,2,1,0:T(8,128)} %bitcast.7, f32[1,2]{1,0:T(1,128)S(1)} %copy-done.5, s32[1]{0:T(128)S(6)} %copy.11.src_ref, s32[1,1024]{1,0:T(1,128)S(1)} %copy-done.2, f32[1,1024]{1,0:T(1,128)S(1)} %copy-done.3, ...), custom_call_target="tpu_custom_call" | custom-call | tf_op jit(solution)/shard_map/shot_terms/pallas_call | solution.py:439
  51.1 22.8 %scatter_slabs.1 = f32[64,4,128]{2,1,0:T(4,128)S(1)} custom-call(f32[16,64,4,128]{3,2,1,0:T(4,128)S(1)} %shot_terms.1.term_ref), custom_call_target="tpu_custom_call" | custom-call | tf_op jit(solution)/shard_map/scatter_slabs/pallas_call | solution.py:144
  74.0 0.7 copy.12
Async XLA Ops:
  0.7 0.9 %copy-start.1 = (f32[4,16,4,128]{3,2,1,0:T(4,128)S(1)}, f32[4,16,4,128]{3,2,1,0:T(4,128)}, u32[]{:S(2)}) copy-start(f32[4,16,4,128]{3,2,1,0:T(4,128)} %param.15) | copy-start | bytes 393220
  25.2 1.0 %copy-start = (s32[16,64,128]{2,1,0:T(8,128)S(1)}, s32[16,64,128]{2,1,0:T(8,128)}, u32[]{:S(2)}) copy-start(s32[16,64,128]{2,1,0:T(8,128)} %class_ref.1) | copy-start | bytes 1572868
  26.2 0.7 copy-start.2
  26.9 0.7 copy-start.3
  27.6 0.7 copy-start.4
  28.3 0.7 copy-start.5

commit v2 on v1

v2 whole, which is shorter than its diff:
```python
import functools

import jax
import jax.numpy as jnp
from jax import lax
from jax.experimental import pallas as pl
from jax.experimental.pallas import tpu as pltpu
from jax.sharding import PartitionSpec as P

BIOT_COEFF = 0.8
RHO_BULK = 2.2
RHO_FLUID = 1.0
MASS_FLUID = 2.5
TIME_STEP = 0.25
DET = RHO_BULK * MASS_FLUID - RHO_FLUID * RHO_FLUID
C_M = TIME_STEP * MASS_FLUID / DET
C_A = TIME_STEP * RHO_BULK / DET
C_B = TIME_STEP * RHO_FLUID / DET

VX, VZ, VY, QX, QZ, QY, SXX, SZZ, SYY, SXZ, SXY, SZY, PR = range(13)
MESH = pl.DeviceIdType.MESH
F32 = jnp.float32


def coordinates(n):
    me = lax.axis_index("shot")
    return lax.rem(me, 2), lax.rem(me // 2, 2), me // 4, n // 4


def index_of(z, y, core):
    return (z * 2 + y) * 2 + core


class Window:
    def __init__(self, x, z0, zc, nz, ny):
        self.x, self.z0, self.zc, self.nz = x, z0, zc, nz
        self.row = lax.broadcasted_iota(jnp.int32, (zc, ny), 0)
        self.lane = lax.broadcasted_iota(jnp.int32, (zc, ny), 1)
        self.ny = ny
        self.seen = {}

    def at(self, ref, f, dx=0, dz=0):
        key = (id(ref), f, dx, dz)
        if key in self.seen:
            return self.seen[key]
        plane = self.x + 1 + dx
        lo = self.z0 + dz
        if lo < 0:
            value = self.at(ref, f, dx)
            value = jnp.where(self.row == 0, 0.0, pltpu.roll(value, 1, 0))
        elif lo + self.zc > self.nz:
            value = self.at(ref, f, dx)
            value = jnp.where(self.row == self.zc - 1, 0.0, pltpu.roll(value, self.zc - 1, 0))
        else:
            value = ref[f, plane, lo:lo + self.zc, :]
        self.seen[key] = value
        return value

    def fx(self, ref, f):
        return self.at(ref, f, 1) - self.at(ref, f)

    def bx(self, ref, f):
        return self.at(ref, f) - self.at(ref, f, -1)

    def fz(self, ref, f):
        return self.at(ref, f, 0, 1) - self.at(ref, f)

    def bz(self, ref, f):
        return self.at(ref, f) - self.at(ref, f, 0, -1)

    def fy(self, ref, f):
        value = self.at(ref, f)
        return jnp.where(self.lane == self.ny - 1, 0.0, pltpu.roll(value, self.ny - 1, 1)) - value

    def by(self, ref, f):
        value = self.at(ref, f)
        return value - jnp.where(self.lane == 0, 0.0, pltpu.roll(value, 1, 1))

    def put(self, ref, f, value):
        ref[f, self.x + 1, self.z0:self.z0 + self.zc, :] = value


STAGES = 7


def kernel(n, zc, fwd_hbm, adj_hbm, amp_hbm, src_hbm, rec_hbm, obs_hbm, own_hbm, class_hbm, cf_hbm,
           out_ref, amp_ref, src_ref, rec_ref, obs_in, class_ref, cf_ref, gathered, terms_ref,
           from_core, to_side, from_side, to_line, from_line,
           st, ad, q1, q2, e1, be, bf, mat, grad, cnt, obs,
           fwd_sem, adj_sem, small_sem, own_sem,
           gz_s, gz_r, gy_s, gy_r, gc_s, gc_r, rc_s, rc_r, ry_s, ry_r, rz_s, rz_r):
    planes, nz, ny = class_ref.shape
    chunks, zs = gathered.shape[0], gathered.shape[1]
    per = planes // chunks
    lag = (STAGES - 1) // per
    piece = gathered.shape[6]
    classes = cf_ref.shape[1]
    core, y, z, _ = coordinates(n)
    other_core = {"shot": index_of(z, y, 1 - core)}
    other_side = {"shot": index_of(z, 1 - y, core)}

    def on_line(d):
        return lax.rem(z + d, zs)

    def own_copy(c):
        return pltpu.make_async_copy(own_hbm.at[:, pl.ds(c * per, per)], gathered.at[c, z, y, core], own_sem.at[c])

    def fwd_copy(x):
        return pltpu.make_async_copy(fwd_hbm.at[:, x], st.at[:, x + 1], fwd_sem.at[x])

    def adj_copy(x):
        return pltpu.make_async_copy(adj_hbm.at[:, x], ad.at[:, x + 1], adj_sem.at[x])

    small = [pltpu.make_async_copy(src, dst, small_sem.at[i]) for i, (src, dst) in enumerate((
        (rec_hbm, rec_ref), (obs_hbm, obs_in), (amp_hbm, amp_ref), (src_hbm, src_ref), (cf_hbm, cf_ref),
        (class_hbm, class_ref)))]

    def remote(src, dst, send_sem, recv_sem, target):
        return pltpu.make_async_remote_copy(
            src_ref=src, dst_ref=dst, send_sem=send_sem, recv_sem=recv_sem, device_id=target, device_id_type=MESH)

    def gather_line(c, d):
        slab = gathered.at[c, z, y, core]
        return remote(slab, slab, gz_s.at[d - 1, c], gz_r.at[d - 1, c], {"shot": index_of(on_line(d), y, core)})

    def gather_side(c):
        slabs = gathered.at[c, :, y, core]
        return remote(slabs, slabs, gy_s.at[c], gy_r.at[c], other_side)

    def gather_core(c):
        slabs = gathered.at[c, :, :, core]
        return remote(slabs, slabs, gc_s.at[c], gc_r.at[c], other_core)

    def reduce_core(c):
        return remote(terms_ref.at[c, :, :, 1 - core], from_core.at[c], rc_s.at[c], rc_r.at[c], other_core)

    def reduce_side(c):
        return remote(to_side.at[c], from_side.at[c], ry_s.at[c], ry_r.at[c], other_side)

    def reduce_line(c, d):
        return remote(to_line.at[c, d - 1], from_line.at[c, d - 1], rz_s.at[d - 1, c], rz_r.at[d - 1, c],
                      {"shot": index_of(on_line(d), y, core)})

    def within(c, step):
        @pl.when(jnp.logical_and(c >= 0, c < chunks))
        def _():
            step(c)

    def gather_0(c):
        own_copy(c).wait()
        for d in range(1, zs):
            gather_line(c, d).start()

    def gather_1(c):
        for d in range(1, zs):
            gather_line(c, d).wait_recv()
        gather_side(c).start()

    def gather_2(c):
        gather_side(c).wait_recv()
        gather_core(c).start()

    def gather_3(c):
        gather_core(c).wait_recv()

    def reduce_0(c):
        reduce_core(c).start()

    def reduce_1(c):
        reduce_core(c).wait_recv()
        for s in range(zs):
            to_side[c, s] = terms_ref[c, s, 1 - y, core] + from_core[c, s, 1 - y]
        reduce_side(c).start()

    def reduce_2(c):
        reduce_side(c).wait_recv()
        for d in range(1, zs):
            s = on_line(d)
            to_line[c, d - 1] = terms_ref[c, s, y, core] + from_core[c, s, y] + from_side[c, s]
            reduce_line(c, d).start()

    def reduce_3(c):
        total = terms_ref[c, z, y, core] + from_core[c, z, y] + from_side[c, z]
        for d in range(1, zs):
            reduce_line(c, d).wait_recv()
            total = total + from_line[c, d - 1]
        out_ref[:, pl.ds(c * per, per)] = total

    for c in range(chunks):
        own_copy(c).start()
    for copy in small:
        copy.start()
    for x in range(planes):
        fwd_copy(x).start()
    for x in range(planes):
        adj_copy(x).start()

    barrier = pltpu.get_barrier_semaphore()
    for target in [other_core, other_side] + [{"shot": index_of(on_line(d), y, core)} for d in range(1, zs)]:
        pl.semaphore_signal(barrier, inc=1, device_id=target, device_id_type=MESH)
    zero_plane = jnp.zeros((nz, ny), F32)
    for ref in (st, q1, q2, be, bf):
        for f in range(ref.shape[0]):
            ref[f, 0] = zero_plane
            ref[f, planes + 1] = zero_plane
    pl.semaphore_wait(barrier, zs + 1)

    ahead = min(3, chunks)
    for c in range(ahead):
        gather_0(c)
    for copy in small:
        copy.wait()

    cells = rec_ref[...]
    rows = lax.div(cells, jnp.int32(ny))
    lanes = cells - rows * ny
    count = cells.shape[1]
    value = obs_in[...]
    hi = value.astype(jnp.bfloat16).astype(F32)
    mid = (value - hi).astype(jnp.bfloat16).astype(F32)
    low = value - hi - mid
    hit = lax.broadcasted_iota(jnp.int32, (ny, count), 0) == lanes
    columns = jnp.concatenate(
        [jnp.where(hit, part, 0.0).astype(jnp.bfloat16) for part in (jnp.ones_like(value), hi, mid, low)], axis=0)

    def place_receivers(x, carry):
        at_row = lax.broadcasted_iota(jnp.int32, (nz, count), 0) + x * nz == rows
        product = lax.dot_general(
            jnp.where(at_row, 1.0, 0.0).astype(jnp.bfloat16), columns, (((1,), (1,)), ((), ())),
            preferred_element_type=F32)
        cnt[x] = product[:, :ny]
        obs[x] = product[:, ny:2 * ny] + product[:, 2 * ny:3 * ny] + product[:, 3 * ny:]
        return carry

    gather_1(0)
    lax.fori_loop(0, planes, place_receivers, 0)
    gather_2(0)
    if chunks > 1:
        gather_1(1)

    def factor_of(k, cls):
        factor = jnp.full(cls.shape, cf_ref[k, classes - 1], F32)
        for c in range(classes - 1):
            factor = jnp.where(cls == c, cf_ref[k, c], factor)
        return factor

    scales = (TIME_STEP, 2.0 * TIME_STEP, TIME_STEP, 1.0)

    source = src_ref[0]
    L, U, B, D = range(4)

    def velocities(q_old, base, q_new, w):
        damp = w.at(mat, D)
        forces = (
            w.fx(st, SXX) + w.bz(st, SXZ) + w.by(st, SXY),
            w.bx(st, SXZ) + w.fz(st, SZZ) + w.by(st, SZY),
            w.bx(st, SXY) + w.bz(st, SZY) + w.fy(st, SYY))
        slopes = (w.fx(st, PR), w.fz(st, PR), w.fy(st, PR))
        for i in range(3):
            flux = w.at(q_old, base + i)
            pull = slopes[i] + damp * flux
            w.put(st, VX + i, w.at(st, VX + i) + (C_M * forces[i] + C_B * pull))
            w.put(q_new, i, flux - (C_A * pull + C_B * forces[i]))

    def strains(q, w):
        exx, ezz, eyy = w.bx(st, VX), w.bz(st, VZ), w.by(st, VY)
        dv = exx + ezz + eyy
        g = BIOT_COEFF * dv + (w.bx(q, 0) + w.bz(q, 1) + w.by(q, 2))
        gxz = w.fz(st, VX) + w.fx(st, VZ)
        gxy = w.fy(st, VX) + w.fx(st, VY)
        gzy = w.fy(st, VZ) + w.fz(st, VY)
        return exx, ezz, eyy, gxz, gxy, gzy, dv, g

    def add_source(w, section, pressure):
        here = (w.row + (w.x * nz + w.z0)) * ny + w.lane == source
        return pressure + jnp.where(here, amp_ref[0, section], 0.0)

    def correlate(w, bars, bar_p, terms):
        exx, ezz, eyy, gxz, gxy, gzy, dv, g = terms
        trace = bars[0] + bars[1] + bars[2]
        aside = BIOT_COEFF * trace - bar_p
        g_lame = trace * dv
        g_shear = 2.0 * (bars[0] * exx + bars[1] * ezz + bars[2] * eyy) + (
            bars[3] * gxz + bars[4] * gxy + bars[5] * gzy)
        g_biot = g * aside
        h = w.at(mat, B) * aside
        common = w.at(mat, L) * trace + BIOT_COEFF * h
        shear2 = w.at(mat, U)
        shear1 = 0.5 * shear2
        for i in range(3):
            w.put(be, i, shear2 * bars[i] + common)
            w.put(be, 3 + i, shear1 * bars[3 + i])
        w.put(be, 6, h)
        return g_lame, g_shear, g_biot

    def bar_motion(w):
        vels = (
            w.at(ad, VX) - (w.fx(be, 0) + w.bz(be, 3) + w.by(be, 4)),
            w.at(ad, VZ) - (w.fz(be, 1) + w.bx(be, 3) + w.by(be, 5)),
            w.at(ad, VY) - (w.fy(be, 2) + w.bx(be, 4) + w.bz(be, 5)))
        fluxes = (
            w.at(ad, QX) - w.fx(be, 6), w.at(ad, QZ) - w.fz(be, 6), w.at(ad, QY) - w.fy(be, 6))
        return vels, fluxes

    def rows_of(ref, k, w):
        return ref[k, w.x, w.z0:w.z0 + zc, :]


    def build_plane(c, j, x):
        cls = class_ref[x]
        for k in range(4):
            for d in range(n):
                mat[k, x + 1, d * piece:(d + 1) * piece, :] = gathered[c, d // 4, d // 2 % 2, d % 2, k, j]
            mat[k, x + 1] = mat[k, x + 1] * factor_of(k, cls) * scales[k]

    def stresses(w):
        terms = strains(q1, w)
        exx, ezz, eyy, gxz, gxy, gzy, dv, g = terms
        bg = w.at(mat, B) * g
        bulk = w.at(mat, L) * dv + BIOT_COEFF * bg
        shear2 = w.at(mat, U)
        shear1 = 0.5 * shear2
        for i, e in enumerate((exx, ezz, eyy)):
            w.put(st, SXX + i, w.at(st, SXX + i) + (shear2 * e + bulk))
        for i, e in enumerate((gxz, gxy, gzy)):
            w.put(st, SXZ + i, w.at(st, SXZ + i) + shear1 * e)
        w.put(st, PR, add_source(w, 0, w.at(st, PR) - bg))
        for i, e in enumerate((exx, ezz, eyy, gxz, gxy, gzy, g)):
            e1[i, w.x, w.z0:w.z0 + zc, :] = e

    def turn(w):
        terms = strains(q2, w)
        final = add_source(w, 1, w.at(st, PR) - w.at(mat, B) * terms[7])
        here = slice(w.z0, w.z0 + zc)
        bar_p = w.at(ad, PR) + (cnt[w.x, here, :] * final - obs[w.x, here, :])
        w.put(ad, PR, bar_p)
        parts = correlate(w, [w.at(ad, SXX + i) for i in range(6)], bar_p, terms)
        for k in range(3):
            grad[k, w.x, here, :] = parts[k]

    def back_motion(w):
        vels, fluxes = bar_motion(w)
        damp = w.at(mat, D)
        total = None
        for i in range(3):
            bar_f = C_M * vels[i] - C_B * fluxes[i]
            bar_r = C_A * fluxes[i] - C_B * vels[i]
            w.put(bf, i, bar_f)
            w.put(bf, 3 + i, bar_r)
            part = w.at(q1, i) * bar_r
            total = part if total is None else total + part
            w.put(ad, VX + i, vels[i])
            w.put(ad, QX + i, fluxes[i] - damp * bar_r)
        grad[3, w.x, w.z0:w.z0 + zc, :] = total

    def back_stress(w):
        bars = (
            w.at(ad, SXX) - w.bx(bf, 0),
            w.at(ad, SZZ) - w.bz(bf, 1),
            w.at(ad, SYY) - w.by(bf, 2),
            w.at(ad, SXZ) - (w.fz(bf, 0) + w.fx(bf, 1)),
            w.at(ad, SXY) - (w.fy(bf, 0) + w.fx(bf, 2)),
            w.at(ad, SZY) - (w.fy(bf, 1) + w.fz(bf, 2)))
        bar_p = w.at(ad, PR) + (w.bx(bf, 3) + w.bz(bf, 4) + w.by(bf, 5))
        terms = [rows_of(e1, i, w) for i in range(6)]
        terms += [terms[0] + terms[1] + terms[2], rows_of(e1, 6, w)]
        parts = correlate(w, bars, bar_p, terms)
        for k in range(3):
            grad[k, w.x, w.z0:w.z0 + zc, :] = rows_of(grad, k, w) + parts[k]

    root = float(n) ** 0.5
    signs = (TIME_STEP / root, TIME_STEP / root, TIME_STEP / root, -1.0 / root)

    def finish(w):
        vels, fluxes = bar_motion(w)
        damp = rows_of(grad, 3, w)
        for i in range(3):
            damp = damp + w.at(st, QX + i) * (C_A * fluxes[i] - C_B * vels[i])
        cls = class_ref[w.x, w.z0:w.z0 + zc, :]
        for k in range(4):
            total = damp if k == 3 else rows_of(grad, k, w)
            total = total * (factor_of(k, cls) * signs[k])
            for r in range(0, zc, piece):
                d = (w.z0 + r) // piece
                terms_ref[w.x // per, d // 4, d // 2 % 2, d % 2, k, w.x % per] = total[r:r + piece]

    stages = (
        functools.partial(velocities, st, QX, q1), stresses, functools.partial(velocities, q1, 0, q2),
        turn, back_motion, back_stress, finish)
    fwd_copy(0).wait()

    def plane_step(c, j):
        t = c * per + j

        @pl.when(t + 1 < planes)
        def _():
            fwd_copy(t + 1).wait()

        @pl.when(t < planes)
        def _():
            build_plane(c, j, t)

        for s, stage in enumerate(stages):
            x = t - s

            @pl.when(jnp.logical_and(x >= 0, x < planes))
            def _():
                if s == 3:
                    adj_copy(x).wait()
                for z0 in range(0, nz, zc):
                    stage(Window(x, z0, zc, nz, ny))

    def chunk_step(c, carry):
        within(c + 3, gather_0)
        within(c + 2, gather_1)
        within(c + 1, gather_2)
        within(c, gather_3)

        def inner(j, inner_carry):
            plane_step(c, j)
            return inner_carry

        lax.fori_loop(0, per, inner, 0)
        done = c - lag
        within(done, reduce_0)
        within(done - 1, reduce_1)
        within(done - 2, reduce_2)
        within(done - 3, reduce_3)
        return carry

    lax.fori_loop(0, chunks + lag, chunk_step, 0)
    last = chunks - 1
    reduce_1(last)
    if last >= 1:
        reduce_2(last - 1)
    reduce_2(last)
    for c in range(max(0, last - 2), chunks):
        reduce_3(c)

    def settle(c, carry):
        for d in range(1, zs):
            gather_line(c, d).wait_send()
            reduce_line(c, d).wait_send()
        for copy in (gather_side(c), gather_core(c), reduce_core(c), reduce_side(c)):
            copy.wait_send()
        return carry

    lax.fori_loop(0, chunks, settle, 0)


def per_device(forward_state, adjoint_state, source_amp, source_cell, receiver_cells, recorded, material,
               cell_class, class_factors):
    n = lax.axis_size("shot")
    params, planes, piece, ny = material.shape
    fields, _, nz, _ = forward_state.shape[1:]
    per = 2 if planes % 2 == 0 else 1
    chunks, zs = planes // per, n // 4
    block = (params, per, piece, ny)
    hbm = pl.BlockSpec(memory_space=pltpu.HBM)
    vmem = lambda *shape: pltpu.VMEM(shape, F32)
    padded = lambda f: vmem(f, planes + 2, nz, ny)
    plain = lambda f: vmem(f, planes, nz, ny)
    dma = pltpu.SemaphoreType.DMA
    return pl.pallas_call(
        functools.partial(kernel, n, 8),
        out_shape=jax.ShapeDtypeStruct(material.shape, F32),
        in_specs=[hbm] * 9,
        out_specs=pl.BlockSpec(memory_space=pltpu.VMEM),
        scratch_shapes=[
            pltpu.SMEM(source_amp.shape, F32), pltpu.SMEM(source_cell.shape, jnp.int32),
            pltpu.VMEM(receiver_cells.shape, jnp.int32), pltpu.VMEM(recorded.shape, F32),
            pltpu.VMEM(cell_class.shape, jnp.int32), pltpu.SMEM(class_factors.shape, F32),
            vmem(chunks, zs, 2, 2, *block), vmem(chunks, zs, 2, 2, *block),
            vmem(chunks, zs, 2, *block), vmem(chunks, zs, *block), vmem(chunks, zs, *block),
            vmem(chunks, zs - 1, *block), vmem(chunks, zs - 1, *block),
            padded(fields), padded(fields), padded(3), padded(3), plain(7), padded(7), padded(6), padded(4), plain(4),
            vmem(planes, nz, ny), vmem(planes, nz, ny),
            dma((planes,)), dma((planes,)), dma((6,)), dma((chunks,)),
            dma((zs - 1, chunks)), dma((zs - 1, chunks)), dma((chunks,)), dma((chunks,)), dma((chunks,)), dma((chunks,)),
            dma((chunks,)), dma((chunks,)), dma((chunks,)), dma((chunks,)), dma((zs - 1, chunks)), dma((zs - 1, chunks))],
        compiler_params=pltpu.CompilerParams(
            collective_id=0, has_side_effects=True, vmem_limit_bytes=60 << 20),
        name="gradient",
    )(forward_state[0], adjoint_state[0], source_amp, source_cell, receiver_cells, recorded, material,
      cell_class, class_factors)


def solution(mesh):
    placed = (
        P(("groups", "shot"), None, None, None, None),
        P(("groups", "shot"), None, None, None, None),
        P(("groups", "shot"), None),
        P(("groups", "shot")),
        P(("groups", "shot"), None),
        P(("groups", "shot"), None),
        P(None, "groups", "shot", None),
        P("groups", None, None),
        P(),
    )
    return jax.shard_map(
        per_device, mesh=mesh, in_specs=placed, out_specs=P(None, "groups", "shot", None), check_vma=False)
```

time: 74.9 us -> 64.5 us (0.86)
  Pallas kernels: 68.6 us -> 62.1 us
  local copies, waits for them, and re-layouts: 5.3 us -> 1.57 us
    pallas_call x3 -> x1, Pallas kernels: 68.6 us -> 62.1 us  [per_device(): pl.pallas_call(functools.partial(kernel, n, 8), out_shape=jax.ShapeDtypeS...]
    unnamed x13 -> x1, local copies, waits for them, and re-layouts: 5.3 us -> 1.57 us
where the time goes in v2:
time: 64.5 us; the launch traced here: 64.4 us
  Pallas kernels  62.1 us (96%)
  local copies, waits for them, and re-layouts  1.57 us (2%)
  between operations  0.66 us (1%)
    pallas_call x1, Pallas kernels, per_device(): pl.pallas_call(functools.partial(kernel, n, 8), out_shape=jax.ShapeDtypeS...  62.1 us
    unnamed x1, local copies, waits for them, and re-layouts  1.57 us

profile of v2, /device:TPU:0, one launch (start us, length us, event | category | flops | bytes accessed | tf_op | source)
XLA Modules:
  0.0 64.4 jit_solution(6893667417154850196)
XLA Ops:
  0.7 62.1 %gradient.1 = f32[4,16,4,128]{3,2,1,0:T(4,128)} custom-call(f32[13,16,64,128]{3,2,1,0:T(8,128)} %bitcast.2, f32[13,16,64,128]{3,2,1,0:T(8,128)} %bitcast.3, f32[1,2]{1,0:T(1,128)} %amp_hbm.1, s32[1]{0:T(128)S(6)} %copy.11.src_hbm, s32[1,1024]{1,0:T(1,128)} %rec_hbm.1, f32[1,1024]{1,0:T(1,128)} %obs_hbm.1, f32[4,16,4,128]{3,2,1,0:T(4,128)} %own_hbm.1, ...), custom_call_target="tpu_custom_call" | custom-call | tf_op jit(solution)/shard_map/gradient/pallas_call | solution.py:464
  62.8 1.6 %copy.12 = f32[4,16,4,128]{3,2,1,0:T(4,128)} copy(f32[4,16,4,128]{3,2,1,0:T(4,128)} %gradient.1) | data formatting | bytes 262144

commit v3 on v2

--- a/solution.py
+++ b/solution.py
@@ -81,6 +81,8 @@
 
 
 STAGES = 7
+GATHER_LEAD = (6, 3, 1)
+REDUCE_LAG = (1, 3, 5)
 
 
 def kernel(n, zc, fwd_hbm, adj_hbm, amp_hbm, src_hbm, rec_hbm, obs_hbm, own_hbm, class_hbm, cf_hbm,
@@ -92,7 +94,7 @@
     planes, nz, ny = class_ref.shape
     chunks, zs = gathered.shape[0], gathered.shape[1]
     per = planes // chunks
-    lag = (STAGES - 1) // per
+    lag = -(-(STAGES - 1) // per)
     piece = gathered.shape[6]
     classes = cf_ref.shape[1]
     core, y, z, _ = coordinates(n)
@@ -205,9 +207,15 @@
             ref[f, planes + 1] = zero_plane
     pl.semaphore_wait(barrier, zs + 1)
 
-    ahead = min(3, chunks)
-    for c in range(ahead):
-        gather_0(c)
+    gathers = (gather_0, gather_1, gather_2)
+
+    def lead_in(first, last):
+        for v in range(first, last):
+            for step, lead in zip(gathers, GATHER_LEAD):
+                if 0 <= v + lead < chunks:
+                    step(v + lead)
+
+    lead_in(-GATHER_LEAD[0], -GATHER_LEAD[1])
     for copy in small:
         copy.wait()
 
@@ -223,20 +231,21 @@
     columns = jnp.concatenate(
         [jnp.where(hit, part, 0.0).astype(jnp.bfloat16) for part in (jnp.ones_like(value), hi, mid, low)], axis=0)
 
-    def place_receivers(x, carry):
-        at_row = lax.broadcasted_iota(jnp.int32, (nz, count), 0) + x * nz == rows
+    group = 4 if planes % 4 == 0 else 1
+
+    def place_receivers(g, carry):
+        at_row = lax.broadcasted_iota(jnp.int32, (group * nz, count), 0) + g * (group * nz) == rows
         product = lax.dot_general(
             jnp.where(at_row, 1.0, 0.0).astype(jnp.bfloat16), columns, (((1,), (1,)), ((), ())),
             preferred_element_type=F32)
-        cnt[x] = product[:, :ny]
-        obs[x] = product[:, ny:2 * ny] + product[:, 2 * ny:3 * ny] + product[:, 3 * ny:]
+        here = pl.ds(g * group, group)
+        cnt[here] = product[:, :ny].reshape(group, nz, ny)
+        seen = product[:, ny:2 * ny] + product[:, 2 * ny:3 * ny] + product[:, 3 * ny:]
+        obs[here] = seen.reshape(group, nz, ny)
         return carry
 
-    gather_1(0)
-    lax.fori_loop(0, planes, place_receivers, 0)
-    gather_2(0)
-    if chunks > 1:
-        gather_1(1)
+    lax.fori_loop(0, planes // group, place_receivers, 0)
+    lead_in(-GATHER_LEAD[1], 0)
 
     def factor_of(k, cls):
         factor = jnp.full(cls.shape, cf_ref[k, classes - 1], F32)
@@ -410,10 +419,11 @@
                 for z0 in range(0, nz, zc):
                     stage(Window(x, z0, zc, nz, ny))
 
+    reduces = (reduce_1, reduce_2, reduce_3)
+
     def chunk_step(c, carry):
-        within(c + 3, gather_0)
-        within(c + 2, gather_1)
-        within(c + 1, gather_2)
+        for step, lead in zip(gathers, GATHER_LEAD):
+            within(c + lead, step)
         within(c, gather_3)
 
         def inner(j, inner_carry):
@@ -423,19 +433,15 @@
         lax.fori_loop(0, per, inner, 0)
         done = c - lag
         within(done, reduce_0)
-        within(done - 1, reduce_1)
-        within(done - 2, reduce_2)
-        within(done - 3, reduce_3)
+        for step, behind in zip(reduces, REDUCE_LAG):
+            within(done - behind, step)
         return carry
 
     lax.fori_loop(0, chunks + lag, chunk_step, 0)
-    last = chunks - 1
-    reduce_1(last)
-    if last >= 1:
-        reduce_2(last - 1)
-    reduce_2(last)
-    for c in range(max(0, last - 2), chunks):
-        reduce_3(c)
+    for v in range(chunks, chunks + REDUCE_LAG[2]):
+        for step, behind in zip(reduces, REDUCE_LAG):
+            if 0 <= v - behind < chunks:
+                step(v - behind)
 
     def settle(c, carry):
         for d in range(1, zs):

time: 64.5 us -> 48.6 us (0.75)
  Pallas kernels: 62.1 us -> 46.2 us
    pallas_call x1, Pallas kernels: 62.1 us -> 46.2 us  [per_device(): pl.pallas_call(functools.partial(kernel, n, 8), out_shape=jax.ShapeDtypeS...]
where the time goes in v3:
time: 48.6 us; the launch traced here: 48.4 us
  Pallas kernels  46.2 us (95%)
  local copies, waits for them, and re-layouts  1.57 us (3%)
  between operations  0.66 us (1%)
    pallas_call x1, Pallas kernels, per_device(): pl.pallas_call(functools.partial(kernel, n, 8), out_shape=jax.ShapeDtypeS...  46.2 us
    unnamed x1, local copies, waits for them, and re-layouts  1.57 us

profile of v3, /device:TPU:0, one launch (start us, length us, event | category | flops | bytes accessed | tf_op | source)
XLA Modules:
  0.0 48.4 jit_solution(15419825155070713489)
XLA Ops:
  0.7 46.2 %gradient.1 = f32[4,16,4,128]{3,2,1,0:T(4,128)} custom-call(f32[13,16,64,128]{3,2,1,0:T(8,128)} %bitcast.2, f32[13,16,64,128]{3,2,1,0:T(8,128)} %bitcast.3, f32[1,2]{1,0:T(1,128)} %amp_hbm.1, s32[1]{0:T(128)S(6)} %copy.11.src_hbm, s32[1,1024]{1,0:T(1,128)} %rec_hbm.1, f32[1,1024]{1,0:T(1,128)} %obs_hbm.1, f32[4,16,4,128]{3,2,1,0:T(4,128)} %own_hbm.1, ...), custom_call_target="tpu_custom_call" | custom-call | tf_op jit(solution)/shard_map/gradient/pallas_call | solution.py:470
  46.9 1.6 %copy.12 = f32[4,16,4,128]{3,2,1,0:T(4,128)} copy(f32[4,16,4,128]{3,2,1,0:T(4,128)} %gradient.1) | data formatting | bytes 262144

commit v4 on v3

--- a/solution.py
+++ b/solution.py
@@ -468,7 +468,7 @@
     plain = lambda f: vmem(f, planes, nz, ny)
     dma = pltpu.SemaphoreType.DMA
     return pl.pallas_call(
-        functools.partial(kernel, n, 8),
+        functools.partial(kernel, n, 16),
         out_shape=jax.ShapeDtypeStruct(material.shape, F32),
         in_specs=[hbm] * 9,
         out_specs=pl.BlockSpec(memory_space=pltpu.VMEM),

time: 48.6 us -> 47.9 us (0.986)
  Pallas kernels: 46.2 us -> 45.5 us
    pallas_call x1, Pallas kernels: 46.2 us -> 45.5 us  [per_device(): pl.pallas_call(functools.partial(kernel, n, 16), out_shape=jax.ShapeDtype...]
where the time goes in v4:
time: 47.9 us; the launch traced here: 47.7 us
  Pallas kernels  45.5 us (95%)
  local copies, waits for them, and re-layouts  1.57 us (3%)
  between operations  0.66 us (1%)
    pallas_call x1, Pallas kernels, per_device(): pl.pallas_call(functools.partial(kernel, n, 16), out_shape=jax.ShapeDtype...  45.5 us
    unnamed x1, local copies, waits for them, and re-layouts  1.57 us

profile of v4, /device:TPU:0, one launch (start us, length us, event | category | flops | bytes accessed | tf_op | source)
XLA Modules:
  0.0 47.7 jit_solution(13532235528619196377)
XLA Ops:
  0.7 45.5 %gradient.1 = f32[4,16,4,128]{3,2,1,0:T(4,128)} custom-call(f32[13,16,64,128]{3,2,1,0:T(8,128)} %bitcast.2, f32[13,16,64,128]{3,2,1,0:T(8,128)} %bitcast.3, f32[1,2]{1,0:T(1,128)} %amp_hbm.1, s32[1]{0:T(128)S(6)} %copy.11.src_hbm, s32[1,1024]{1,0:T(1,128)} %rec_hbm.1, f32[1,1024]{1,0:T(1,128)} %obs_hbm.1, f32[4,16,4,128]{3,2,1,0:T(4,128)} %own_hbm.1, ...), custom_call_target="tpu_custom_call" | custom-call | tf_op jit(solution)/shard_map/gradient/pallas_call | solution.py:470
  46.2 1.6 %copy.12 = f32[4,16,4,128]{3,2,1,0:T(4,128)} copy(f32[4,16,4,128]{3,2,1,0:T(4,128)} %gradient.1) | data formatting | bytes 262144
